TPU v7x, 32 devices: a whole 2x2x4 slice. The times are simulated.
32 devices in a mesh: row: 8 (over z, core), col: 4 (over y, x).
Axes of the slice: x: 2, y: 2, z: 4, core: 2. Of those that a mesh axis runs over, the one named last changes fastest.
Arguments:
- tile_values: bfloat16 [2048, 128, 128], P(('row', 'col')), may hold values from -0.1875 to 0.1875
- slot_codes: int32 [2048], P(('row', 'col')), may hold values from -1 to 127, as said below
- right_start: float32 [8192, 256], P(('row', 'col')), may hold values from -6 to 6
- left_start: float32 [8192, 256], P(('row', 'col')), may hold values from -6 to 6
- node_diagonal: float32 [8192], P(('row', 'col')), may hold values from 1 to 3
- row_scale: float32 [8192], P(('row', 'col')), may hold values from 0.2 to 15
Outputs:
- right_block: float32 [8192, 256], P(('row', 'col'))
- left_block: float32 [8192, 256], P(('row', 'col'))
- projections: float32 [2, 256, 256], replicated
Inputs may be any that keep to these rules, and one draw needn't show every extreme that they name: `slot_codes`: slot (s, p, c) carries a tile that device s extracted for owner p; its code is -1 (empty) or a position a 16 + b in p's block grid of 8 x 2 * 8 places. The codes of one owner's live slots over all sources are distinct, so an owner receives at most 32 live tiles, and some owner receives exactly 32. A source fills at most 2 slots for one owner, and some source fills all 2.
All inputs are finite; a program needn't handle non-finite values.
Results may differ from a plain program's by a relative error of at most 0.002.
Values may be sent and summed in bfloat16 or wider, within the bound.
No kernel may reach another device: no remote copies, remote signals or barrier semaphores. Data moves between devices by JAX's collectives and lax.ppermute only.
A program may use at most 128 MiB of HBM per device.

v0:
```python
import jax
import jax.numpy as jnp
from jax import lax
from jax.sharding import PartitionSpec as P

ITERS = 2
epsilon = 1e-06


def local(tile_values, slot_codes, right_start, left_start, node_diagonal, row_scale):
    row_size = lax.axis_size("row")
    col_size = lax.axis_size("col")
    owners = row_size * col_size
    tile_rows = tile_values.shape[1]
    order_rows = right_start.shape[0] * owners
    grid_rows = 2 * col_size
    grid_cols = 2 * row_size
    got_tiles, got_codes = (
        lax.all_to_all(tile_values, ("row", "col"), split_axis=0, concat_axis=0, tiled=True),
        lax.all_to_all(slot_codes, ("row", "col"), split_axis=0, concat_axis=0, tiled=True),
    )
    live = got_codes >= 0
    places = grid_rows * grid_cols
    safe_keys = jnp.where(live, got_codes, places)
    region = jnp.zeros((places, tile_rows, tile_rows), jnp.bfloat16)
    region = region.at[safe_keys].set(got_tiles, mode="drop")
    region = region.reshape(grid_rows, grid_cols, tile_rows, tile_rows).transpose(0, 2, 1, 3)
    matrix = region.reshape(grid_rows * tile_rows, grid_cols * tile_rows)
    scale_col = row_scale[:, None]
    diag_col = node_diagonal[:, None]
    right_vec = right_start
    left_vec = right_start + left_start
    stored = []
    for turn in range(ITERS):
        right_bf = right_vec.astype(jnp.bfloat16)
        scaled_left = scale_col * left_vec
        left_bf = scaled_left.astype(jnp.bfloat16)
        right_cols = lax.all_gather(right_bf, "row", axis=0, tiled=True)
        left_rows = lax.all_gather(left_bf, "col", axis=0, tiled=True)
        right_part = jnp.dot(matrix, right_cols, preferred_element_type=jnp.float32)
        left_part = lax.dot_general(
            matrix, left_rows, (((0,), (0,)), ((), ())), preferred_element_type=jnp.float32
        )
        right_prod = lax.psum_scatter(right_part, "col", scatter_dimension=0, tiled=True)
        left_prod = lax.psum_scatter(left_part, "row", scatter_dimension=0, tiled=True)
        right_new = scale_col * (right_prod + diag_col * right_vec)
        left_new = left_prod + diag_col * scaled_left
        local_proj = jnp.dot(left_vec.T, right_new, precision=lax.Precision.HIGHEST)
        project = lax.psum(local_proj, ("row", "col")) / order_rows
        right_rest = right_new - jnp.dot(right_vec, project, precision=lax.Precision.HIGHEST)
        left_rest = left_new - jnp.dot(left_vec, project.T, precision=lax.Precision.HIGHEST)
        right_sq, left_sq = lax.psum(
            (jnp.sum(right_rest * right_rest, axis=0), jnp.sum(left_rest * left_rest, axis=0)),
            ("row", "col"),
        )
        right_vec = right_rest / jnp.sqrt(right_sq / order_rows + epsilon)[None, :]
        left_vec = left_rest / jnp.sqrt(left_sq / order_rows + epsilon)[None, :]
        stored.append(project)
    return (right_vec, left_vec, jnp.stack(stored))


def solution(mesh):
    return jax.shard_map(
        local,
        mesh=mesh,
        in_specs=(
            P(("row", "col"), None, None),
            P(("row", "col")),
            P(("row", "col"), None),
            P(("row", "col"), None),
            P(("row", "col")),
            P(("row", "col")),
        ),
        out_specs=(P(("row", "col"), None), P(("row", "col"), None), P()),
        check_vma=False,
    )
```

profile of v0, /device:TPU:10, one launch (start us, length us, event | category | flops | bytes accessed | tf_op | source)
XLA Modules:
  0.0 619.5 jit_solution(10229374278468693904)
XLA Ops:
  7.2 0.8 all_to_all.11
  8.0 10.9 %all_to_all.17 = s32[32,2,1]{1,2,0:T(1,128)S(1)} all-to-all(s32[32,2,1]{1,2,0:T(1,128)S(1)} %bitcast.37), channel_id=1, replica_groups=mesh['row'=8,'col'=4] {'row','col'}, dimensions={0} | all-to-all | bytes 512 | tf_op jit(solution)/shard_map/all_to_all | solution.py:20
  18.9 4.8 all-to-all-start.1
  25.9 51.8 %all-to-all-done.1 = bf16[64,128,128]{2,1,0:T(8,128)(2,1)S(1)} async-done(((bf16[64,128,128]{2,1,0:T(8,128)(2,1)}), bf16[64,128,128]{2,1,0:T(8,128)(2,1)S(1)}, u32[]{:S(2)}, u32[]{:S(2)}) %all-to-all-start.1) | async-done | bytes 2097184 | tf_op jit(solution)/shard_map/all_to_all | solution.py:19
  77.7 3.0 broadcast_in_dim.6
  80.7 10.7 %scatter_fusion = bf16[128,128,128]{2,1,0:T(8,128)(2,1)} fusion(bf16[128,128,128]{2,1,0:T(8,128)(2,1)} %broadcast_in_dim.6, s32[64]{0:T(128)S(1)} %fusion.27, bf16[64,128,128]{2,1,0:T(8,128)(2,1)S(1)} %all-to-all-done.1), kind=kCustom, calls=%fused_computation | custom fusion | bytes 6291712 | tf_op jit(solution)/shard_map/scatter | solution.py:26
  91.4 6.8 %copy.11 = bf16[8,16,128,128]{3,1,2,0:T(8,128)(2,1)} copy(bf16[8,16,128,128]{3,2,1,0:T(8,128)(2,1)} %bitcast.32) | data formatting | bytes 8388608 | tf_op jit(solution)/shard_map/reshape | solution.py:27
  98.3 4.7 fusion.6
  103.1 15.5 %all_gather.14 = bf16[1024,256]{1,0:T(8,128)(2,1)S(1)} all-gather(bf16[256,256]{1,0:T(8,128)(2,1)S(1)} %get-tuple-element.7), channel_id=1, replica_groups=mesh['row'=8,'col'=4] {'col'}, dimensions={0}, use_global_device_ids=true | all-gather | bytes 655360 | tf_op jit(solution)/shard_map/all_gather | solution.py:39
  118.6 15.7 %reduce-scatter.5.cloned.1.call-done = f32[256,256]{1,0:T(8,128)} async-done(((f32[1024,256]{1,0:T(8,128)}), f32[256,256]{1,0:T(8,128)}) %reduce-scatter.5.cloned.1.call-update) | async-done | bytes 262160 | tf_op jit(solution)/shard_map/reduce_scatter | solution.py:44
  134.3 2.3 fusion.17
  136.7 5.6 fusion.2
  142.3 124.6 %all-reduce.5.cloned.1.call-done = f32[256,256]{1,0:T(8,128)} async-done(((f32[256,256]{1,0:T(8,128)}), f32[256,256]{1,0:T(8,128)}) %all-reduce.5.cloned.1.call-update) | async-done | bytes 262160 | tf_op jit(solution)/shard_map/psum | solution.py:49
  266.9 1.4 multiply_reduce_fusion.3
  268.3 32.0 %reduce-scatter.9.cloned.1.call-done = f32[256,256]{1,0:T(8,128)} async-done(((f32[2048,256]{1,0:T(8,128)}), f32[256,256]{1,0:T(8,128)}) %reduce-scatter.9.cloned.1.call-update) | async-done | bytes 262160 | tf_op jit(solution)/shard_map/reduce_scatter | solution.py:45
  300.4 1.5 multiply_reduce_fusion.2
  301.8 43.8 %all-reduce.1 = (f32[256]{0:T(256)S(1)}, f32[256]{0:T(256)S(1)}) all-reduce(f32[256]{0:T(256)S(1)} %get-tuple-element.10, f32[256]{0:T(256)S(1)} %get-tuple-element.12), channel_id=1, replica_groups=mesh['row'=8,'col'=4] {'row','col'}, use_global_device_ids=true, to_apply=%region_4.5 | all-reduce | flops 512 | bytes 4096 | tf_op jit(solution)/shard_map/psum | solution.py:52
  346.5 20.5 %all-gather.5.cloned.1.call-done = bf16[2048,256]{1,0:T(8,128)(2,1)} async-done(((bf16[256,256]{1,0:T(8,128)(2,1)}), bf16[2048,256]{1,0:T(8,128)(2,1)}) %all-gather.5.cloned.1.call-update) | async-done | bytes 1048592 | tf_op jit(solution)/shard_map/all_gather | solution.py:38
  367.1 4.7 fusion.4
  372.0 13.6 %all_gather.15 = bf16[1024,256]{1,0:T(8,128)(2,1)S(1)} all-gather(bf16[256,256]{1,0:T(8,128)(2,1)S(1)} %multiply_convert_fusion), channel_id=1, replica_groups=mesh['row'=8,'col'=4] {'col'}, dimensions={0}, use_global_device_ids=true | all-gather | bytes 655360 | tf_op jit(solution)/shard_map/all_gather | solution.py:39
  385.6 14.1 %reduce-scatter.7.cloned.1.call-done = f32[256,256]{1,0:T(8,128)} async-done(((f32[1024,256]{1,0:T(8,128)}), f32[256,256]{1,0:T(8,128)}) %reduce-scatter.7.cloned.1.call-update) | async-done | bytes 262160 | tf_op jit(solution)/shard_map/reduce_scatter | solution.py:44
  399.7 2.3 fusion.18
  402.1 5.6 fusion
  407.7 124.6 %all-reduce.7.cloned.1.call-done = f32[256,256]{1,0:T(8,128)} async-done(((f32[256,256]{1,0:T(8,128)}), f32[256,256]{1,0:T(8,128)}) %all-reduce.7.cloned.1.call-update) | async-done | bytes 262160 | tf_op jit(solution)/shard_map/psum | solution.py:49
  532.4 1.0 multiply_bitcast_fusion
  533.3 0.8 pad_maximum_fusion
  534.2 1.4 multiply_reduce_fusion.1
  535.5 30.5 %reduce-scatter.11.cloned.1.call-done = f32[256,256]{1,0:T(8,128)} async-done(((f32[2048,256]{1,0:T(8,128)}), f32[256,256]{1,0:T(8,128)}) %reduce-scatter.11.cloned.1.call-update) | async-done | bytes 262160 | tf_op jit(solution)/shard_map/reduce_scatter | solution.py:45
  566.1 1.5 multiply_reduce_fusion
  567.5 43.6 %all-reduce = (f32[256]{0:T(256)S(1)}, f32[256]{0:T(256)S(1)}) all-reduce(f32[256]{0:T(256)S(1)} %get-tuple-element.14, f32[256]{0:T(256)S(1)} %get-tuple-element.16), channel_id=1, replica_groups=mesh['row'=8,'col'=4] {'row','col'}, use_global_device_ids=true, to_apply=%region_11.12 | all-reduce | flops 512 | bytes 4096 | tf_op jit(solution)/shard_map/psum | solution.py:52
  611.2 0.7 broadcast_divide_fusion
  611.9 0.7 broadcast_divide_fusion.1
  (42 shorter events, 3.5 us)
Async XLA Ops:
  7.2 16.6 %copy-start.4 = (f32[256]{0:T(256)S(1)}, f32[256]{0:T(256)}, u32[]{:S(2)}) copy-start(f32[256]{0:T(256)} %param.11) | copy-start | bytes 3076
  7.2 16.6 %copy-start.1 = (f32[256,256]{1,0:T(8,128)S(1)}, f32[256,256]{1,0:T(8,128)}, u32[]{:S(2)}) copy-start(f32[256,256]{1,0:T(8,128)} %param.8) | copy-start | bytes 786436
  7.2 16.6 %copy-start.3 = (f32[256,256]{1,0:T(8,128)S(1)}, f32[256,256]{1,0:T(8,128)}, u32[]{:S(2)}) copy-start(f32[256,256]{1,0:T(8,128)} %param.9) | copy-start | bytes 786436
  18.9 58.8 %all-to-all-start.1 = ((bf16[64,128,128]{2,1,0:T(8,128)(2,1)}), bf16[64,128,128]{2,1,0:T(8,128)(2,1)S(1)}, u32[]{:S(2)}, u32[]{:S(2)}) async-start(bf16[64,128,128]{2,1,0:T(8,128)(2,1)} %param.6), calls=%async_computation.1 | async-start | bytes 4194304 | tf_op jit(solution)/shard_map/all_to_all | solution.py:19
  23.7 74.6 %all-gather.3.cloned.1.call-start = ((), (), s32[]{:S(2)}) async-start(), calls=%async_computation.6 | async-start | bytes 1179648 | tf_op jit(solution)/shard_map/all_gather | solution.py:38
  24.5 109.7 %reduce-scatter.5.cloned.1.call-start = ((), (), s32[]{:S(2)}) async-start(), calls=%async_computation.7 | async-start | bytes 1310720 | tf_op jit(solution)/shard_map/reduce_scatter | solution.py:44
  98.3 36.0 %copy-start.5 = (f32[256]{0:T(256)S(1)}, f32[256]{0:T(256)}, u32[]{:S(2)}) copy-start(f32[256]{0:T(256)} %param.10) | copy-start | bytes 3076
  103.0 163.9 %all-reduce.5.cloned.1.call-start = ((), (), s32[]{:S(2)}) async-start(), calls=%async_computation.8 | async-start | bytes 524288 | tf_op jit(solution)/shard_map/psum | solution.py:49
  136.6 130.3 %copy-start.2 = (f32[256,256]{1,0:T(8,128)S(1)}, f32[256,256]{1,0:T(8,128)}, u32[]{:S(2)}) copy-start(f32[256,256]{1,0:T(8,128)} %reduce-scatter.5.cloned.1.call-done) | copy-start | bytes 786436
  136.6 163.7 %reduce-scatter.9.cloned.1.call-start = ((), (), s32[]{:S(2)}) async-start(), calls=%async_computation.11 | async-start | bytes 2359296 | tf_op jit(solution)/shard_map/reduce_scatter | solution.py:45
  142.3 224.8 %all-gather.5.cloned.1.call-start = ((), (), s32[]{:S(2)}) async-start(), calls=%async_computation.9 | async-start | bytes 1179648 | tf_op jit(solution)/shard_map/all_gather | solution.py:38
  346.3 53.4 %reduce-scatter.7.cloned.1.call-start = ((), (), s32[]{:S(2)}) async-start(), calls=%async_computation.10 | async-start | bytes 1310720 | tf_op jit(solution)/shard_map/reduce_scatter | solution.py:44
  371.8 160.6 %all-reduce.7.cloned.1.call-start = ((), (), s32[]{:S(2)}) async-start(), calls=%async_computation.12 | async-start | bytes 524288 | tf_op jit(solution)/shard_map/psum | solution.py:49
  402.0 5.7 copy-start
  402.1 164.0 %reduce-scatter.11.cloned.1.call-start = ((), (), s32[]{:S(2)}) async-start(), calls=%async_computation.13 | async-start | bytes 2359296 | tf_op jit(solution)/shard_map/reduce_scatter | solution.py:45
  407.7 126.5 %copy-start.6 = (f32[256,256]{1,0:T(8,128)S(1)}, f32[256,256]{1,0:T(8,128)}, u32[]{:S(2)}) copy-start(f32[256,256]{1,0:T(8,128)} %reduce-scatter.7.cloned.1.call-done) | copy-start | bytes 786436
Sparse Core Ops, SparseCore 0:
  26.7 30.5 all-gather.2
  103.2 31.0 reduce-scatter.4
  140.3 126.5 all-reduce.4
  269.1 31.2 reduce-scatter.8
  346.4 20.5 all-gather.4
  371.9 27.7 reduce-scatter.6
  405.8 126.5 all-reduce.6
  534.7 31.3 reduce-scatter.10
where the time goes:
time: 621 us; the launch traced here: 619 us
  waiting for transfers between devices  414 us (67%)
  blocking collectives  127 us (20%)
  matrix products  30.9 us (5%)
  local copies, waits for them, and re-layouts  22 us (4%)
  between operations  14.3 us (2%)
    psum x2, waiting for transfers between devices, local(): project = lax.psum(local_proj, ('row', 'col')) / order_rows  249 us
    psum x2, blocking collectives, local(): lax.psum((jnp.sum(right_rest * right_rest, axis=0), jnp.sum(left_rest * l...  87.4 us
    reduce_scatter x2, waiting for transfers between devices, local(): lax.psum_scatter(left_part, 'row', scatter_dimension=0, tiled=True)  62.6 us
    all_to_all x1, waiting for transfers between devices, local(): lax.all_to_all(tile_values, ('row', 'col'), split_axis=0, concat_axis=0,...  51.8 us
    reduce_scatter x2, waiting for transfers between devices, local(): lax.psum_scatter(right_part, 'col', scatter_dimension=0, tiled=True)  29.8 us
    all_gather x2, blocking collectives, local(): left_rows = lax.all_gather(left_bf, 'col', axis=0, tiled=True)  29.1 us
    all_gather x2, waiting for transfers between devices, local(): right_cols = lax.all_gather(right_bf, 'row', axis=0, tiled=True)  20.5 us
  transfers between devices with their start and end apart: 9, of which 8 were waited for; matrix products, arithmetic and copies ran while one was open for 6% of the time, Pallas kernels for 0%

commit v1 on v0

--- a/solution.py
+++ b/solution.py
@@ -46,7 +46,7 @@
         right_new = scale_col * (right_prod + diag_col * right_vec)
         left_new = left_prod + diag_col * scaled_left
         local_proj = jnp.dot(left_vec.T, right_new, precision=lax.Precision.HIGHEST)
-        project = lax.psum(local_proj, ("row", "col")) / order_rows
+        project = jnp.sum(lax.all_gather(local_proj, ("row", "col")), axis=0) / order_rows
         right_rest = right_new - jnp.dot(right_vec, project, precision=lax.Precision.HIGHEST)
         left_rest = left_new - jnp.dot(left_vec, project.T, precision=lax.Precision.HIGHEST)
         right_sq, left_sq = lax.psum(

time: 621 us -> 513 us (0.83)
  waiting for transfers between devices: 414 us -> 313 us
  blocking collectives: 127 us -> 117 us
  other arithmetic: 5.48 us -> 12.5 us
    psum x2 -> x0, waiting for transfers between devices: 249 us -> none  [local(): project = lax.psum(local_proj, ('row', 'col')) / order_rows]
    all_gather x0 -> x2, waiting for transfers between devices: none -> 126 us  [local(): lax.all_gather(local_proj, ('row', 'col'))]
    reduce_scatter x2, waiting for transfers between devices: 29.8 us -> 57.8 us  [local(): lax.psum_scatter(right_part, 'col', scatter_dimension=0, tiled=True)]
    all_gather x2, blocking collectives: 29.1 us -> 18.2 us  [local(): left_rows = lax.all_gather(left_bf, 'col', axis=0, tiled=True)]
    reduce_sum x0 -> x2, other arithmetic: none -> 7.94 us  [local(): jnp.sum(lax.all_gather(local_proj, ('row', 'col')), axis=0) / order_rows]
  transfers between devices with their start and end apart: 9 -> 9, of which waited for: 8 -> 8; matrix products, arithmetic and copies ran while one was open for 6% -> 8% of each run, Pallas kernels for 0% -> 0%
where the time goes in v1:
time: 513 us; the launch traced here: 512 us
  waiting for transfers between devices  313 us (61%)
  blocking collectives  117 us (23%)
  matrix products  29.2 us (6%)
  local copies, waits for them, and re-layouts  20.5 us (4%)
  between operations  14.3 us (3%)
  other arithmetic  12.5 us (2%)
  starting transfers between devices  5.32 us (1%)
    all_gather x2, waiting for transfers between devices, local(): lax.all_gather(local_proj, ('row', 'col'))  126 us
    psum x2, blocking collectives, local(): lax.psum((jnp.sum(right_rest * right_rest, axis=0), jnp.sum(left_rest * l...  87.5 us
    reduce_scatter x2, waiting for transfers between devices, local(): lax.psum_scatter(right_part, 'col', scatter_dimension=0, tiled=True)  57.8 us
    reduce_scatter x2, waiting for transfers between devices, local(): lax.psum_scatter(left_part, 'row', scatter_dimension=0, tiled=True)  56.6 us
    all_to_all x1, waiting for transfers between devices, local(): lax.all_to_all(tile_values, ('row', 'col'), split_axis=0, concat_axis=0,...  51.8 us
    all_gather x2, waiting for transfers between devices, local(): right_cols = lax.all_gather(right_bf, 'row', axis=0, tiled=True)  20.6 us
    all_gather x2, blocking collectives, local(): left_rows = lax.all_gather(left_bf, 'col', axis=0, tiled=True)  18.2 us
    dot_general x2, matrix products, local(): lax.dot_general(matrix, left_rows, (((0,), (0,)), ((), ())), preferred_el...  11.5 us
  transfers between devices with their start and end apart: 9, of which 8 were waited for; matrix products, arithmetic and copies ran while one was open for 8% of the time, Pallas kernels for 0%

profile of v1, /device:TPU:10, one launch (start us, length us, event | category | flops | bytes accessed | tf_op | source)
XLA Modules:
  0.0 511.7 jit_solution(10641434819742502461)
XLA Ops:
  7.2 0.8 all_to_all.11
  8.0 10.9 %all_to_all.17 = s32[32,2,1]{1,2,0:T(1,128)S(1)} all-to-all(s32[32,2,1]{1,2,0:T(1,128)S(1)} %bitcast.41), channel_id=1, replica_groups=mesh['row'=8,'col'=4] {'row','col'}, dimensions={0} | all-to-all | bytes 512 | tf_op jit(solution)/shard_map/all_to_all | solution.py:20
  18.9 4.8 all-to-all-start.1
  23.8 0.7 multiply_convert_fusion.1
  25.9 51.8 %all-to-all-done.1 = bf16[64,128,128]{2,1,0:T(8,128)(2,1)S(1)} async-done(((bf16[64,128,128]{2,1,0:T(8,128)(2,1)}), bf16[64,128,128]{2,1,0:T(8,128)(2,1)S(1)}, u32[]{:S(2)}, u32[]{:S(2)}) %all-to-all-start.1) | async-done | bytes 2097184 | tf_op jit(solution)/shard_map/all_to_all | solution.py:19
  77.7 3.0 broadcast_in_dim.6
  80.7 9.2 %scatter_fusion = bf16[128,128,128]{2,1,0:T(8,128)(2,1)} fusion(bf16[128,128,128]{2,1,0:T(8,128)(2,1)} %broadcast_in_dim.6, s32[64]{0:T(128)S(1)} %fusion.27, bf16[64,128,128]{2,1,0:T(8,128)(2,1)S(1)} %all-to-all-done.1), kind=kCustom, calls=%fused_computation | custom fusion | bytes 6291712 | tf_op jit(solution)/shard_map/scatter | solution.py:26
  89.9 6.9 %copy.11 = bf16[8,16,128,128]{3,1,2,0:T(8,128)(2,1)} copy(bf16[8,16,128,128]{3,2,1,0:T(8,128)(2,1)} %bitcast.34) | data formatting | bytes 8388608 | tf_op jit(solution)/shard_map/reshape | solution.py:27
  96.8 4.8 fusion.6
  101.6 30.3 %reduce-scatter.5.cloned.1.call-done = f32[256,256]{1,0:T(8,128)} async-done(((f32[1024,256]{1,0:T(8,128)}), f32[256,256]{1,0:T(8,128)}) %reduce-scatter.5.cloned.1.call-update) | async-done | bytes 262160 | tf_op jit(solution)/shard_map/reduce_scatter | solution.py:44
  131.9 2.3 fusion.17
  134.3 9.1 %all_gather.28 = bf16[1024,256]{1,0:T(8,128)(2,1)S(1)} all-gather(bf16[256,256]{1,0:T(8,128)(2,1)S(1)} %get-tuple-element.7), channel_id=1, replica_groups=mesh['row'=8,'col'=4] {'col'}, dimensions={0}, use_global_device_ids=true | all-gather | bytes 655360 | tf_op jit(solution)/shard_map/all_gather | solution.py:39
  143.4 5.7 %fusion.2 = f32[2048,256]{1,0:T(8,128)} fusion(bf16[1024,256]{1,0:T(8,128)(2,1)S(1)} %all_gather.28, bf16[128,8,16,128]{3,2,1,0:T(8,128)(2,1)} %bitcast.38), kind=kOutput, calls=%fused_computation.3 | convolution fusion | flops 1073741824 | bytes 6815744 | tf_op jit(solution)/shard_map/dot_general | solution.py:41
  149.2 63.2 %all-gather.11.cloned.1.call-done = f32[8192,256]{1,0:T(8,128)} async-done(((f32[256,256]{1,0:T(8,128)}), f32[8192,256]{1,0:T(8,128)}) %all-gather.11.cloned.1.call-update) | async-done | bytes 8388624 | tf_op jit(solution)/shard_map/all_gather | solution.py:49
  212.5 4.0 reduce_sum.54
  216.9 28.7 %reduce-scatter.9.cloned.1.call-done = f32[256,256]{1,0:T(8,128)} async-done(((f32[2048,256]{1,0:T(8,128)}), f32[256,256]{1,0:T(8,128)}) %reduce-scatter.9.cloned.1.call-update) | async-done | bytes 262160 | tf_op jit(solution)/shard_map/reduce_scatter | solution.py:45
  245.5 1.4 multiply_reduce_fusion.2
  246.9 43.8 %all-reduce.1 = (f32[256]{0:T(256)S(1)}, f32[256]{0:T(256)S(1)}) all-reduce(f32[256]{0:T(256)S(1)} %get-tuple-element.10, f32[256]{0:T(256)S(1)} %get-tuple-element.12), channel_id=1, replica_groups=mesh['row'=8,'col'=4] {'row','col'}, use_global_device_ids=true, to_apply=%region_4.5 | all-reduce | flops 512 | bytes 4096 | tf_op jit(solution)/shard_map/psum | solution.py:52
  291.6 20.6 %all-gather.9.cloned.1.call-done = bf16[2048,256]{1,0:T(8,128)(2,1)} async-done(((bf16[256,256]{1,0:T(8,128)(2,1)}), bf16[2048,256]{1,0:T(8,128)(2,1)}) %all-gather.9.cloned.1.call-update) | async-done | bytes 1048592 | tf_op jit(solution)/shard_map/all_gather | solution.py:38
  312.2 4.7 fusion.4
  317.0 27.5 %reduce-scatter.7.cloned.1.call-done = f32[256,256]{1,0:T(8,128)} async-done(((f32[1024,256]{1,0:T(8,128)}), f32[256,256]{1,0:T(8,128)}) %reduce-scatter.7.cloned.1.call-update) | async-done | bytes 262160 | tf_op jit(solution)/shard_map/reduce_scatter | solution.py:44
  344.6 2.3 fusion.18
  347.1 9.1 %all_gather.31 = bf16[1024,256]{1,0:T(8,128)(2,1)S(1)} all-gather(bf16[256,256]{1,0:T(8,128)(2,1)S(1)} %multiply_convert_fusion), channel_id=1, replica_groups=mesh['row'=8,'col'=4] {'col'}, dimensions={0}, use_global_device_ids=true | all-gather | bytes 655360 | tf_op jit(solution)/shard_map/all_gather | solution.py:39
  356.2 5.7 %fusion = f32[2048,256]{1,0:T(8,128)} fusion(bf16[1024,256]{1,0:T(8,128)(2,1)S(1)} %all_gather.31, bf16[128,8,16,128]{3,2,1,0:T(8,128)(2,1)} %bitcast.40), kind=kOutput, calls=%fused_computation.1 | convolution fusion | flops 1073741824 | bytes 6815744 | tf_op jit(solution)/shard_map/dot_general | solution.py:41
  361.9 63.1 %all-gather.13.cloned.1.call-done = f32[8192,256]{1,0:T(8,128)} async-done(((f32[256,256]{1,0:T(8,128)}), f32[8192,256]{1,0:T(8,128)}) %all-gather.13.cloned.1.call-update) | async-done | bytes 8388624 | tf_op jit(solution)/shard_map/all_gather | solution.py:49
  425.1 4.0 reduce_sum.57
  429.1 0.8 pad_maximum_fusion
  430.3 28.0 %reduce-scatter.11.cloned.1.call-done = f32[256,256]{1,0:T(8,128)} async-done(((f32[2048,256]{1,0:T(8,128)}), f32[256,256]{1,0:T(8,128)}) %reduce-scatter.11.cloned.1.call-update) | async-done | bytes 262160 | tf_op jit(solution)/shard_map/reduce_scatter | solution.py:45
  458.3 1.4 multiply_reduce_fusion
  459.7 43.8 %all-reduce = (f32[256]{0:T(256)S(1)}, f32[256]{0:T(256)S(1)}) all-reduce(f32[256]{0:T(256)S(1)} %get-tuple-element.14, f32[256]{0:T(256)S(1)} %get-tuple-element.16), channel_id=1, replica_groups=mesh['row'=8,'col'=4] {'row','col'}, use_global_device_ids=true, to_apply=%region_11.12 | all-reduce | flops 512 | bytes 4096 | tf_op jit(solution)/shard_map/psum | solution.py:52
  503.4 0.7 broadcast_divide_fusion
  504.2 0.7 broadcast_divide_fusion.1
  (42 shorter events, 3.7 us)
Async XLA Ops:
  7.2 16.6 %copy-start.3 = (f32[256]{0:T(256)S(1)}, f32[256]{0:T(256)}, u32[]{:S(2)}) copy-start(f32[256]{0:T(256)} %param.11) | copy-start | bytes 3076
  7.2 16.6 %copy-start = (f32[256,256]{1,0:T(8,128)S(1)}, f32[256,256]{1,0:T(8,128)}, u32[]{:S(2)}) copy-start(f32[256,256]{1,0:T(8,128)} %param.8) | copy-start | bytes 786436
  7.2 16.6 %copy-start.2 = (f32[256,256]{1,0:T(8,128)S(1)}, f32[256,256]{1,0:T(8,128)}, u32[]{:S(2)}) copy-start(f32[256,256]{1,0:T(8,128)} %param.9) | copy-start | bytes 786436
  18.9 58.8 %all-to-all-start.1 = ((bf16[64,128,128]{2,1,0:T(8,128)(2,1)}), bf16[64,128,128]{2,1,0:T(8,128)(2,1)S(1)}, u32[]{:S(2)}, u32[]{:S(2)}) async-start(bf16[64,128,128]{2,1,0:T(8,128)(2,1)} %param.6), calls=%async_computation.1 | async-start | bytes 4194304 | tf_op jit(solution)/shard_map/all_to_all | solution.py:19
  23.7 73.0 %all-gather.7.cloned.1.call-start = ((), (), s32[]{:S(2)}) async-start(), calls=%async_computation.6 | async-start | bytes 1179648 | tf_op jit(solution)/shard_map/all_gather | solution.py:38
  24.5 107.4 %reduce-scatter.5.cloned.1.call-start = ((), (), s32[]{:S(2)}) async-start(), calls=%async_computation.7 | async-start | bytes 1310720 | tf_op jit(solution)/shard_map/reduce_scatter | solution.py:44
  96.8 35.2 %copy-start.4 = (f32[256]{0:T(256)S(1)}, f32[256]{0:T(256)}, u32[]{:S(2)}) copy-start(f32[256]{0:T(256)} %param.10) | copy-start | bytes 3076
  101.5 110.9 %all-gather.11.cloned.1.call-start = ((), (), s32[]{:S(2)}) async-start(), calls=%async_computation.12 | async-start | bytes 8650752 | tf_op jit(solution)/shard_map/all_gather | solution.py:49
  134.3 111.2 %reduce-scatter.9.cloned.1.call-start = ((), (), s32[]{:S(2)}) async-start(), calls=%async_computation.10 | async-start | bytes 2359296 | tf_op jit(solution)/shard_map/reduce_scatter | solution.py:45
  149.2 163.1 %all-gather.9.cloned.1.call-start = ((), (), s32[]{:S(2)}) async-start(), calls=%async_computation.8 | async-start | bytes 1179648 | tf_op jit(solution)/shard_map/all_gather | solution.py:38
  212.4 4.0 copy-start.1
  291.4 53.2 %reduce-scatter.7.cloned.1.call-start = ((), (), s32[]{:S(2)}) async-start(), calls=%async_computation.9 | async-start | bytes 1310720 | tf_op jit(solution)/shard_map/reduce_scatter | solution.py:44
  317.0 108.1 %all-gather.13.cloned.1.call-start = ((), (), s32[]{:S(2)}) async-start(), calls=%async_computation.13 | async-start | bytes 8650752 | tf_op jit(solution)/shard_map/all_gather | solution.py:49
  346.9 111.4 %reduce-scatter.11.cloned.1.call-start = ((), (), s32[]{:S(2)}) async-start(), calls=%async_computation.11 | async-start | bytes 2359296 | tf_op jit(solution)/shard_map/reduce_scatter | solution.py:45
  425.1 4.8 copy-start.5
Sparse Core Ops, SparseCore 0:
  26.7 30.5 all-gather.6
  101.7 30.2 reduce-scatter.4
  135.4 77.0 all-gather.10
  214.6 30.8 reduce-scatter.8
  291.5 20.6 all-gather.8
  317.1 27.4 reduce-scatter.6
  348.0 77.0 all-gather.12
  427.4 30.8 reduce-scatter.10
